TPU v7x, 1024 devices: a whole 4x8x16 slice. The times are simulated.
1024 devices in a mesh: lat: 32 (over x, y), lev: 32 (over z, core).
Axes of the slice: x: 4, y: 8, z: 16, core: 2. Of those that a mesh axis runs over, the one named last changes fastest.
Arguments:
- grid_gradient: float32 [64, 640, 1280], P('lev', 'lat'), may hold values from -0.4375 to 0.4375
- legendre: bfloat16 [640, 640, 320], P('lat', 'lev'), may hold values from -0.15625 to 0.15625
- assign: int32 [640], replicated, may hold values from 0 to 639, as said below
Outputs:
- coeff_gradient: bfloat16 [640, 640, 128], P('lat', 'lev')
Inputs may be any that keep to these rules, and one draw needn't show every extreme that they name: `assign`: each wavenumber appears once; slots 2q and 2q + 1 hold two wavenumbers that sum to 639.
All inputs are finite; a program needn't handle non-finite values.
Results may differ from a plain program's by a relative error of at most 0.0059.
Values may be sent and summed in bfloat16 or wider, within the bound.
A program may use at most 32 MiB of HBM per device.

v0:
```python
import math

import jax
import jax.numpy as jnp
from jax import lax
from jax.sharding import PartitionSpec as P


def split_halves(arrived, half):
    north = arrived[..., :half].astype(jnp.float32)
    south = arrived[..., ::-1][..., :half].astype(jnp.float32)
    return ((north + south).astype(jnp.bfloat16), (north - south).astype(jnp.bfloat16))


def per_device(grid_gradient, legendre, assign):
    fl_dev, rows, nlon = grid_gradient.shape
    modes = nlon // 2
    slots_dev, deg_dev, half = legendre.shape
    lat_id = lax.axis_index("lat")
    lev_id = lax.axis_index("lev")
    longitudes = jnp.arange(nlon, dtype=jnp.int32)
    phase = longitudes[:, None] * assign[None, :] % nlon
    angle = phase.astype(jnp.float32) * (2.0 * math.pi / nlon)
    weight = jnp.where(assign == 0, 1.0, 2.0).astype(jnp.float32)
    table = jnp.stack([jnp.cos(angle) * weight, -jnp.sin(angle) * weight], axis=1)
    spec = jnp.einsum(
        "lcs,frl->sfcr",
        table,
        grid_gradient,
        precision=lax.Precision.HIGHEST,
        preferred_element_type=jnp.float32,
    ).astype(jnp.bfloat16)
    arrived = lax.all_to_all(spec, "lat", split_axis=0, concat_axis=3, tiled=True)
    mine = lax.dynamic_slice(assign, (lat_id * slots_dev,), (slots_dev,))
    paired = legendre.reshape(slots_dev, deg_dev // 2, 2, half)
    piece = lax.all_gather(arrived, "lev", axis=1, tiled=True)
    even, odd = split_halves(piece, half)
    from_even = jnp.einsum(
        "str,sfcr->stcf", paired[:, :, 0], even, preferred_element_type=jnp.float32
    )
    from_odd = jnp.einsum(
        "str,sfcr->stcf", paired[:, :, 1], odd, preferred_element_type=jnp.float32
    )
    both = jnp.stack([from_even, from_odd], axis=2)
    columns = both.reshape(slots_dev, deg_dev, 2, piece.shape[1])
    degrees = lev_id * deg_dev + jnp.arange(deg_dev, dtype=jnp.int32)
    valid = degrees[None, :] < (modes - mine)[:, None]
    result = jnp.where(valid[:, :, None, None], columns, 0.0).astype(jnp.bfloat16)
    return result.reshape(slots_dev, deg_dev, result.shape[2] * result.shape[3])


def solution(mesh):
    in_specs = (P("lev", "lat", None), P("lat", "lev", None), P())
    out_specs = P("lat", "lev", None)
    return jax.shard_map(
        per_device, mesh=mesh, in_specs=in_specs, out_specs=out_specs, check_vma=False
    )
```

profile of v0, /device:TPU:1, one launch (start us, length us, event | category | flops | bytes accessed | tf_op | source)
XLA Modules:
  0.0 155.0 jit_solution(11978156807525584112)
XLA Ops:
  6.5 0.0 all-gather.2.cloned.1.call-start
  6.5 0.7 compare_select_fusion
  7.2 0.0 copy-start.3
  7.2 14.2 %cosine_multiply_fusion = (f32[1280,1,640]{2,0,1:T(8,128)S(1)}, f32[1280,1,640]{2,0,1:T(8,128)S(1)}) fusion(f32[640]{0:T(1024)S(1)} %compare_select_fusion, s32[640]{0:T(1024)} %param.5), kind=kLoop, calls=%fused_computation.12 | loop fusion | flops 9830400 | bytes 6558720 | tf_op jit(solution)/shard_map/mul | solution.py:25
  21.5 0.0 copy-done.3
  21.5 4.2 %fusion.23 = bf16[640,2,2,20]{0,3,1,2:T(8,128)(2,1)S(1)} fusion(f32[1280,1,640]{2,0,1:T(8,128)S(1)} %get-tuple-element.10, f32[1280,1,640]{2,0,1:T(8,128)S(1)} %get-tuple-element.9, f32[2,20,1280]{2,0,1:T(2,128)S(1)} %copy-done.3), kind=kOutput, calls=%fused_computation.24 | convolution fusion | flops 788121600 | bytes 6860800 | tf_op jit(solution)/shard_map/lcs,frl->sfcr/dot_general | solution.py:26
  25.7 0.0 copy-start.2
  25.7 0.9 copy.32
  26.7 0.8 reshape.165
  27.5 19.6 %all_to_all.18 = bf16[32,2,800]{2,1,0:T(2,128)(2,1)S(1)} all-to-all(bf16[32,2,800]{2,1,0:T(2,128)(2,1)S(1)} %reshape.165), channel_id=1, replica_groups=mesh['lat'=32,'lev'=32] {'lat'}, dimensions={0} | all-to-all | bytes 204800 | tf_op jit(solution)/shard_map/all_to_all | solution.py:33
  47.0 0.6 reshape.166
  47.6 0.2 copy.71
  47.8 1.3 all_to_all.16
  49.1 0.7 copy.35
  49.8 0.0 all-gather.2.cloned.1.call-update
  49.8 0.0 copy-done.2
  49.8 0.2 reshape.159
  50.1 0.8 dynamic-slice_subtract_fusion
  50.8 0.1 broadcast_compare_fusion
  50.9 0.4 fusion.28
  51.3 78.3 %all-gather.2.cloned.1.call-done = bf16[20,64,2,640]{3,2,0,1:T(2,128)(2,1)} async-done(((bf16[20,2,2,640]{3,2,0,1:T(2,128)(2,1)}), bf16[20,64,2,640]{3,2,0,1:T(2,128)(2,1)}) %all-gather.2.cloned.1.call-update) | async-done | bytes 3276816 | tf_op jit(solution)/shard_map/all_gather | solution.py:36
  129.7 6.8 %fusion.27 = (bf16[20,64,2,320]{3,2,0,1:T(2,128)(2,1)}, bf16[20,64,2,320]{3,2,0,1:T(2,128)(2,1)S(1)}) fusion(bf16[20,64,2,640]{3,2,0,1:T(2,128)(2,1)} %all-gather.2.cloned.1.call-done), kind=kLoop, calls=%fused_computation.37 | loop fusion | bytes 6553600 | tf_op jit(solution)/shard_map/slice | solution.py:10
  136.5 0.4 copy.47
  136.8 5.4 %reverse.1 = bf16[20,64,2,384]{3,1,2,0:T(8,128)(2,1)} reverse(bf16[20,64,2,384]{3,1,2,0:T(8,128)(2,1)S(1)} %bitcast.44), dimensions={3} | reverse | bytes 3932160
  142.3 0.0 copy-start
  142.3 0.0 copy-start.1
  142.3 3.5 %fusion.19 = bf16[20,10,1,2,64]{4,1,3,0,2:T(8,128)(2,1)S(1)} fusion(bf16[20,64,2,320]{3,2,0,1:T(2,128)(2,1)} %get-tuple-element.5, bf16[20,10,1,320]{3,2,1,0:T(2,128)(2,1)S(1)} %get-tuple-element.8, bf16[20,64,2,384]{3,1,2,0:T(8,128)(2,1)} %reverse.1), kind=kOutput, calls=%fused_computation.22 | convolution fusion | flops 19660800 | bytes 3783680 | tf_op jit(solution)/shard_map/str,sfcr->stcf/dot_general | solution.py:41
  145.8 0.0 copy-done
  145.8 0.0 copy-done.1
  145.8 1.2 fusion.16
  147.0 0.1 pad_maximum_fusion
  147.1 0.2 copy.40
  147.3 0.1 reshape.160
  147.4 0.8 select_convert_fusion
Async XLA Ops:
  6.5 123.1 %all-gather.2.cloned.1.call-start = ((), (), s32[]{:S(2)}) async-start(), calls=%async_computation.1 | async-start | bytes 3379200 | tf_op jit(solution)/shard_map/all_gather | solution.py:36
  7.2 14.3 %copy-start.3 = (f32[2,20,1280]{2,0,1:T(2,128)S(1)}, f32[2,20,1280]{2,0,1:T(2,128)}, u32[]{:S(2)}) copy-start(f32[2,20,1280]{2,0,1:T(2,128)} %param.3) | copy-start | bytes 614404
  25.7 24.1 %copy-start.2 = (bf16[20,20,320]{2,1,0:T(8,128)(2,1)S(1)}, bf16[20,20,320]{2,1,0:T(8,128)(2,1)}, u32[]{:S(2)}) copy-start(bf16[20,20,320]{2,1,0:T(8,128)(2,1)} %param.4) | copy-start | bytes 768004
  142.3 3.5 %copy-start = (bf16[20,64,2,384]{3,1,2,0:T(8,128)(2,1)S(1)}, bf16[20,64,2,384]{3,1,2,0:T(8,128)(2,1)}, u32[]{:S(2)}) copy-start(bf16[20,64,2,384]{3,1,2,0:T(8,128)(2,1)} %reverse.1) | copy-start | bytes 5898244
  142.3 3.5 %copy-start.1 = (bf16[20,64,2,320]{3,2,0,1:T(2,128)(2,1)S(1)}, bf16[20,64,2,320]{3,2,0,1:T(2,128)(2,1)}, u32[]{:S(2)}) copy-start(bf16[20,64,2,320]{3,2,0,1:T(2,128)(2,1)} %get-tuple-element.5) | copy-start | bytes 4915204
Sparse Core Ops, SparseCore 0:
  49.9 79.6 all-gather.1
where the time goes:
time: 155 us
  waiting for transfers between devices  78.3 us (51%)
  blocking collectives  19.6 us (13%)
  local copies, waits for them, and re-layouts  18 us (12%)
  other arithmetic  16.7 us (11%)
  between operations  13.5 us (9%)
  matrix products  8.93 us (6%)
    all_gather x1, waiting for transfers between devices, per_device(): piece = lax.all_gather(arrived, 'lev', axis=1, tiled=True)  78.3 us
    all_to_all x1, blocking collectives, per_device(): lax.all_to_all(spec, 'lat', split_axis=0, concat_axis=3, tiled=True)  19.6 us
    mul x1, other arithmetic, per_device(): jnp.cos(angle) * weight  14.2 us
    unnamed x12, local copies, waits for them, and re-layouts  7.21 us
    slice x1, local copies, waits for them, and re-layouts, split_halves(): north = arrived[..., :half].astype(jnp.float32)  6.78 us
    dot_general x1, matrix products, per_device(): jnp.einsum('lcs,frl->sfcr', table, grid_gradient, precision=lax.Precision...  4.23 us
    dot_general x1, matrix products, per_device(): jnp.einsum('str,sfcr->stcf', paired[:, :, 1], odd, preferred_element_type...  3.5 us
  transfers between devices with their start and end apart: 1, of which 1 were waited for; matrix products, arithmetic and copies ran while one was open for 1% of the time, Pallas kernels for 0%

commit v1 on v0

v1 whole, which is shorter than its diff:
```python
import functools

import jax
import jax.numpy as jnp
import numpy as np
from jax import lax
from jax.experimental import pallas as pl
from jax.experimental.pallas import tpu as pltpu
from jax.sharding import PartitionSpec as P

MESH = pl.DeviceIdType.MESH
LANES = 128
ROWS = 20
HALF = 10
KAPPA = 5
PAIRS = HALF // 2
DEG = 24
NT = (((1,), (1,)), ((), ()))


def dot_nt(a, b):
    return lax.dot_general(a, b, NT, preferred_element_type=jnp.float32)


def dot(a, b):
    return jnp.dot(a, b, preferred_element_type=jnp.float32)


def iota(shape, axis):
    return lax.broadcasted_iota(jnp.int32, shape, axis)


def kernel(
    n_lat, n_z, g_ref, leg_ref, asg_ref, tab_hbm, out_ref,
    tab, grid, spec, asg_col, send32, send, recv, mixed, leg32, w_own, w_send, w_part, units, first, p_send, p_recv,
    tab_sem, a_send_sem, a_recv_sem, local_sem, w_sems, p_sems, u_send_sem, u_recv_sem,
):
    modes = n_lat * ROWS
    wide = modes
    half = wide // 2
    dests = 2 * n_lat
    lat = lax.axis_index("lat")
    lev = lax.axis_index("lev")
    z, core = lev // 2, lev % 2
    other = 1 - core
    right = ((z + 1) % n_z) * 2 + core
    left = ((z + n_z - 1) % n_z) * 2 + core
    partner = z * 2 + other
    me = lat * 2 + core

    barrier = pltpu.get_barrier_semaphore()

    def greet(target_lat, target_lev):
        pl.semaphore_signal(barrier, inc=1, device_id={"lat": target_lat, "lev": target_lev}, device_id_type=MESH)

    greet(lat, right)
    greet(lat, left)
    greet(lat, partner)

    def greet_all(step, carry):
        target = (lat + step) % n_lat
        greet(target, z * 2)
        greet(target, z * 2 + 1)
        return carry

    lax.fori_loop(1, n_lat, greet_all, 0)

    quarter = modes // 2
    tab_copies = []
    for i in range(4):
        rows = pl.ds(i * quarter, quarter)
        copy = pltpu.make_async_copy(tab_hbm.at[rows], tab.at[rows], tab_sem.at[i])
        copy.start()
        tab_copies.append(copy)

    for f in range(2):
        value = g_ref[f]
        high = value.astype(jnp.bfloat16).astype(jnp.float32)
        grid[f * DEG : f * DEG + ROWS, :] = high
        grid[64 + f * DEG : 64 + f * DEG + ROWS, :] = value - high
    both = grid[...].astype(jnp.bfloat16)

    for t in range(asg_ref.shape[0]):
        row = jnp.broadcast_to(asg_ref[t : t + 1, :].astype(jnp.float32), (LANES, LANES))
        asg_col[t * LANES : (t + 1) * LANES, :] = jnp.transpose(row)

    for i in range(4):
        tab_copies[i].wait()
        part = dot_nt(tab[i * quarter : (i + 1) * quarter, :], both)
        total = part + pltpu.roll(part, 64, 1)
        c, r = i // 2, (i % 2) * quarter
        spec[r : r + quarter, c * LANES : (c + 1) * LANES] = total.astype(jnp.bfloat16)

    picked = 2 * dests
    lane = iota((picked, LANES), 1)
    tiles = -(-modes // LANES)
    mode_of = iota((picked, modes), 1).astype(jnp.float32)
    packed = [[jnp.zeros((picked, LANES), jnp.float32) for _ in range(2)] for _ in range(2)]
    for kappa in range(KAPPA):
        wave = asg_col[pl.ds(kappa, picked, stride=KAPPA), :]
        wave = jnp.concatenate([wave] * tiles, axis=1)[:, :modes]
        choice = jnp.where(wave == mode_of, 1.0, 0.0).astype(jnp.bfloat16)
        chosen = dot(choice, spec[...])
        here = (lane >= kappa * ROWS) & (lane < (kappa + 1) * ROWS)
        for f in range(2):
            for c in range(2):
                moved = chosen[:, c * LANES : (c + 1) * LANES]
                shift = (kappa * ROWS - f * DEG) % LANES
                if shift:
                    moved = pltpu.roll(moved, shift, 1)
                packed[f][c] = jnp.where(here, moved, packed[f][c])
    for f in range(2):
        for c in range(2):
            send32[pl.ds(f * 2 + c, picked, stride=4), :] = packed[f][c]
    send[...] = send32[...].reshape(dests, 8, LANES).astype(jnp.bfloat16)

    pl.semaphore_wait(barrier, 2 * n_lat - 1 + 2)

    def block_to(target_lat, h):
        pltpu.make_async_remote_copy(
            src_ref=send.at[target_lat * 2 + h],
            dst_ref=recv.at[me],
            send_sem=a_send_sem,
            recv_sem=a_recv_sem,
            device_id={"lat": target_lat, "lev": z * 2 + h},
            device_id_type=MESH,
        ).start()

    def blocks_to(step, carry):
        target = (lat + step) % n_lat
        block_to(target, 0)
        block_to(target, 1)
        return carry

    lax.fori_loop(1, n_lat, blocks_to, 0)
    block_to(lat, other)
    own_block = pltpu.make_async_copy(send.at[me], recv.at[me], local_sem)
    own_block.start()

    for s in range(ROWS):
        leg32[s * DEG : s * DEG + ROWS, :] = leg_ref[s].astype(jnp.float32)
    row_of = iota((half, wide), 0)
    col_of = iota((half, wide), 1)
    mirror = jnp.where((row_of == col_of) | (row_of + col_of == wide - 1), 1.0, 0.0).astype(jnp.bfloat16)
    degree = iota((DEG, wide), 0)
    sign = jnp.where((degree % 2 == 1) & (iota((DEG, wide), 1) >= half), -1.0, 1.0)
    degree = degree.astype(jnp.float32)

    def factors(h, p, ref):
        pair = []
        first_slot = h * HALF + 2 * p
        source = leg32[pl.ds(pl.multiple_of(first_slot * DEG, 8), 2 * DEG), :].astype(jnp.bfloat16)
        spread = dot(source, mirror)
        for s in range(2):
            wave = asg_col[pl.ds(lat * ROWS + first_slot + s, 1), :]
            wave = jnp.concatenate([wave] * tiles, axis=1)[:, :modes]
            limit = jnp.minimum(modes - wave - (lev * ROWS).astype(jnp.float32), float(ROWS))
            keep = degree < jnp.broadcast_to(limit, (DEG, wide))
            pair.append(jnp.where(keep, spread[s * DEG : (s + 1) * DEG] * sign, 0.0))
        ref[p] = jnp.concatenate(pair, axis=0).astype(jnp.bfloat16)

    for p in range(PAIRS):
        factors(other, p, w_send)
    w_copy = pltpu.make_async_remote_copy(
        src_ref=w_send, dst_ref=w_part, send_sem=w_sems.at[0], recv_sem=w_sems.at[1],
        device_id={"lat": lat, "lev": partner}, device_id_type=MESH,
    )
    w_copy.start()
    for p in range(PAIRS):
        factors(core, p, w_own)

    src = iota((n_z * 16, 2 * n_z * 8), 0)
    dst = iota((n_z * 16, 2 * n_z * 8), 1)
    position, inner = src // 16, src % 16
    away = (position + 1) // 2
    from_z = jnp.where(position % 2 == 1, z - away + n_z, z + away) % n_z
    field = from_z * 4 + (inner % 8) // 2
    column = (inner // 8) * (n_z * 8) + (inner % 2) * (n_z * 4) + field
    place = jnp.where(column == dst, 1.0, 0.0).astype(jnp.bfloat16)

    pltpu.make_async_copy(recv.at[pl.ds(0, dests - 1)], recv.at[pl.ds(0, dests - 1)], a_recv_sem).wait()
    own_block.wait()
    low = iota((8, LANES), 0) < 4
    for i in range(n_lat):
        a = recv[2 * i].astype(jnp.float32)
        b = recv[2 * i + 1].astype(jnp.float32)
        mixed[0, i] = jnp.where(low, a, pltpu.roll(b, 4, 0))
        mixed[1, i] = jnp.where(low, pltpu.roll(a, 4, 0), b)

    lane = iota((8, LANES), 1)

    def side_by_side(slot):
        u, kappa = slot // KAPPA, slot % KAPPA
        parts = [jnp.zeros((8, LANES), jnp.float32) for _ in range(tiles)]
        for i in range(n_lat):
            start = i * ROWS
            t, offset = start // LANES, start % LANES
            value = mixed[u, i]
            shift = (offset - kappa * ROWS) % LANES
            if shift:
                value = pltpu.roll(value, shift, 1)
            parts[t] = jnp.where((lane >= offset) & (lane < offset + ROWS), value, parts[t])
            if offset + ROWS > LANES:
                parts[t + 1] = jnp.where(lane < offset + ROWS - LANES, value, parts[t + 1])
        return jnp.concatenate(parts, axis=1)[:, :wide]

    def unit_copy(source, target, p, device):
        rows = pl.ds(p * 16, 16)
        return pltpu.make_async_remote_copy(
            src_ref=units.at[source, rows],
            dst_ref=units.at[target, rows],
            send_sem=u_send_sem,
            recv_sem=u_recv_sem.at[target, p],
            device_id={"lat": lat, "lev": device},
            device_id_type=MESH,
        )

    last = n_z - 1

    def pass_right(step, p):
        source = 0 if step == 0 else 2 * step - 1
        if step + 1 < n_z // 2:
            unit_copy(source, 2 * step + 1, p, right).start()
        elif step + 1 == n_z // 2 and p < 3:
            unit_copy(source, last, p, right).start()

    def pass_left(step, p):
        source = 2 * step
        if step + 1 < n_z // 2:
            unit_copy(source, 2 * step + 2, p, left).start()
        elif step + 1 == n_z // 2 and p >= 3:
            unit_copy(source, last, p, left).start()

    for p in range(PAIRS):
        rows = jnp.concatenate([side_by_side(2 * p), side_by_side(2 * p + 1)], axis=0)
        units[0, p * 16 : (p + 1) * 16, :] = rows.astype(jnp.bfloat16)
        pass_right(0, p)
        pass_left(0, p)

    w_copy.wait()

    def contract(p, begin, end):
        arrived = units[begin:end, p * 16 : (p + 1) * 16, :].reshape((end - begin) * 16, wide)
        factor = jnp.concatenate([w_own[p], w_part[p]], axis=0)
        return dot_nt(factor, arrived).astype(jnp.bfloat16)

    middle = n_z // 2
    for step in range(1, n_z // 2):
        for p in range(PAIRS):
            unit_copy(0, 2 * step - 1, p, right).wait_recv()
            pass_right(step, p)
            unit_copy(0, 2 * step, p, left).wait_recv()
            pass_left(step, p)
            if step == n_z // 4:
                first[p] = contract(p, 0, middle)
    for p in range(PAIRS):
        unit_copy(0, last, p, right).wait_recv()
        second = contract(p, middle, n_z)
        product = dot(jnp.concatenate([first[p], second], axis=1), place)
        width = n_z * 8
        for s in range(2):
            lanes = slice(s * width, (s + 1) * width)
            mine = product[s * DEG : s * DEG + ROWS, lanes].astype(jnp.bfloat16)
            out_ref[core * HALF + 2 * p + s] = mine
            theirs = product[(2 + s) * DEG : (3 + s) * DEG, lanes].astype(jnp.bfloat16)
            p_send[2 * p + s] = theirs

    p_copy = pltpu.make_async_remote_copy(
        src_ref=p_send, dst_ref=p_recv, send_sem=p_sems.at[0], recv_sem=p_sems.at[1],
        device_id={"lat": lat, "lev": partner}, device_id_type=MESH,
    )
    p_copy.start()
    pltpu.make_async_copy(send.at[pl.ds(0, dests - 1)], send.at[pl.ds(0, dests - 1)], a_send_sem).wait()
    pltpu.make_async_copy(units.at[pl.ds(0, last)], units.at[pl.ds(0, last)], u_send_sem).wait()
    p_copy.wait()
    for s in range(HALF):
        out_ref[other * HALF + s] = p_recv[s][:ROWS, :]


def table_of(modes, nlon):
    phase = np.arange(modes, dtype=np.int64)[:, None] * np.arange(nlon, dtype=np.int64)[None, :] % nlon
    angle = phase * (2.0 * np.pi / nlon)
    weight = np.where(np.arange(modes) == 0, 1.0, 2.0)[:, None]
    return np.concatenate([np.cos(angle) * weight, -np.sin(angle) * weight], axis=0)


def per_device(n_lat, n_z, grid_gradient, legendre, assign):
    modes = n_lat * ROWS
    nlon = grid_gradient.shape[2]
    wide, half, dests = modes, modes // 2, 2 * n_lat
    tiles = -(-modes // LANES)
    table = jnp.asarray(table_of(modes, nlon).astype(jnp.bfloat16))
    rows = jnp.pad(assign, (0, tiles * LANES - modes)).reshape(tiles, LANES)
    vmem = pl.BlockSpec(memory_space=pltpu.VMEM)
    bf16, f32 = jnp.bfloat16, jnp.float32
    dma = pltpu.SemaphoreType.DMA
    return pl.pallas_call(
        functools.partial(kernel, n_lat, n_z),
        out_shape=jax.ShapeDtypeStruct((ROWS, ROWS, n_z * 8), bf16),
        in_specs=[vmem, vmem, vmem, pl.BlockSpec(memory_space=pltpu.MemorySpace.HBM)],
        out_specs=vmem,
        scratch_shapes=[
            pltpu.VMEM((2 * modes, nlon), bf16),
            pltpu.VMEM((LANES, nlon), f32),
            pltpu.VMEM((modes, 2 * LANES), bf16),
            pltpu.VMEM((tiles * LANES, LANES), f32),
            pltpu.VMEM((dests * 8, LANES), f32),
            pltpu.VMEM((dests, 8, LANES), bf16),
            pltpu.VMEM((dests, 8, LANES), bf16),
            pltpu.VMEM((2, n_lat, 8, LANES), f32),
            pltpu.VMEM((ROWS * DEG, half), f32),
            pltpu.VMEM((PAIRS, 2 * DEG, wide), bf16),
            pltpu.VMEM((PAIRS, 2 * DEG, wide), bf16),
            pltpu.VMEM((PAIRS, 2 * DEG, wide), bf16),
            pltpu.VMEM((n_z, HALF * 8, wide), bf16),
            pltpu.VMEM((PAIRS, 4 * DEG, n_z * 8), bf16),
            pltpu.VMEM((HALF, DEG, n_z * 8), bf16),
            pltpu.VMEM((HALF, DEG, n_z * 8), bf16),
            dma((4,)),
            dma,
            dma,
            dma,
            dma((2,)),
            dma((2,)),
            dma,
            dma((n_z, PAIRS)),
        ],
        compiler_params=pltpu.CompilerParams(collective_id=0, has_side_effects=True),
        name="spectral_adjoint",
    )(grid_gradient, legendre, rows, table)


def solution(mesh):
    in_specs = (P("lev", "lat", None), P("lat", "lev", None), P())
    out_specs = P("lat", "lev", None)
    body = functools.partial(per_device, mesh.shape["lat"], mesh.shape["lev"] // 2)
    return jax.shard_map(body, mesh=mesh, in_specs=in_specs, out_specs=out_specs, check_vma=False)
```

time: 155 us -> 67.2 us (0.43)
  waiting for transfers between devices: 78.3 us -> 0 us
  Pallas kernels: 0 us -> 63.8 us
  blocking collectives: 19.6 us -> 0 us
  other arithmetic: 16.7 us -> 0 us
  local copies, waits for them, and re-layouts: 18 us -> 3.19 us
  between operations: 13.5 us -> 0.01 us
  matrix products: 8.93 us -> 0 us
    all_gather x1 -> x0, waiting for transfers between devices: 78.3 us -> none  [per_device(): piece = lax.all_gather(arrived, 'lev', axis=1, tiled=True)]
    pallas_call x0 -> x1, Pallas kernels: none -> 63.8 us  [per_device(): pl.pallas_call(functools.partial(kernel, n_lat, n_z), out_shape=jax.Shape...]
    all_to_all x1 -> x0, blocking collectives: 19.6 us -> none  [per_device(): lax.all_to_all(spec, 'lat', split_axis=0, concat_axis=3, tiled=True)]
    mul x1 -> x0, other arithmetic: 14.2 us -> none  [per_device(): jnp.cos(angle) * weight]
    dot_general x3 -> x0, matrix products: 8.93 us -> none  [the longest x1 4.23 us: per_device(): jnp.einsum('lcs,frl->sfcr', table, grid_gradient, precision=lax.Precision...]
    slice x2 -> x0, local copies, waits for them, and re-layouts: 7.21 us -> none  [the longest x1 6.78 us: split_halves(): north = arrived[..., :half].astype(jnp.float32)]
    unnamed x12 -> x2, local copies, waits for them, and re-layouts: 7.21 us -> 3.19 us
    all_to_all x3 -> x0, local copies, waits for them, and re-layouts: 2.16 us -> none  [per_device(): lax.all_to_all(spec, 'lat', split_axis=0, concat_axis=3, tiled=True)]
  transfers between devices with their start and end apart: 1 -> 0, of which waited for: 1 -> 0; matrix products, arithmetic and copies ran while one was open for 1% -> 0% of each run, Pallas kernels for 0% -> 0%
where the time goes in v1:
time: 67.2 us; the launch traced here: 67 us
  Pallas kernels  63.8 us (95%)
  local copies, waits for them, and re-layouts  3.19 us (5%)
    pallas_call x1, Pallas kernels, per_device(): pl.pallas_call(functools.partial(kernel, n_lat, n_z), out_shape=jax.Shape...  63.8 us
    unnamed x2, local copies, waits for them, and re-layouts  3.19 us

profile of v1, /device:TPU:1, one launch (start us, length us, event | category | flops | bytes accessed | tf_op | source)
XLA Modules:
  0.0 67.0 jit_solution(13447348753177481968)
XLA Ops:
  0.0 1.6 %copy.5.g_ref = f32[2,20,1280]{2,1,0:T(8,128)} copy(f32[2,20,1280]{2,0,1:T(2,128)} %param.4) | data formatting | bytes 409600 | tf_op args[0]
  1.6 63.8 %spectral_adjoint.1 = bf16[20,20,128]{2,1,0:T(8,128)(2,1)} custom-call(f32[2,20,1280]{2,1,0:T(8,128)} %copy.5.g_ref, bf16[20,20,320]{2,1,0:T(8,128)(2,1)} %leg_ref.1, s32[5,128]{1,0:T(8,128)} %bitcast.1, bf16[1280,1280]{1,0:T(8,128)(2,1)} %constant.1.clone.tab_hbm), custom_call_target="tpu_custom_call" | custom-call | tf_op jit(solution)/shard_map/spectral_adjoint/pallas_call | solution.py:297
  65.4 1.6 %copy.7 = bf16[20,20,128]{2,1,0:T(8,128)(2,1)} copy(bf16[20,20,128]{2,1,0:T(8,128)(2,1)} %spectral_adjoint.1) | data formatting | bytes 204800

commit v2 on v1

--- a/solution.py
+++ b/solution.py
@@ -32,12 +32,13 @@
 
 def kernel(
     n_lat, n_z, g_ref, leg_ref, asg_ref, tab_hbm, out_ref,
-    tab, grid, spec, asg_col, send32, send, recv, mixed, leg32, w_own, w_send, w_part, units, first, p_send, p_recv,
+    tab, grid, both, spec, asg_col, send32, send, recv, mixed, leg32, w_own, w_send, w_part, units, first, p_send, p_recv,
     tab_sem, a_send_sem, a_recv_sem, local_sem, w_sems, p_sems, u_send_sem, u_recv_sem,
 ):
     modes = n_lat * ROWS
     wide = modes
     half = wide // 2
+    nlon = tab.shape[1]
     dests = 2 * n_lat
     lat = lax.axis_index("lat")
     lev = lax.axis_index("lev")
@@ -65,40 +66,51 @@
 
     lax.fori_loop(1, n_lat, greet_all, 0)
 
-    quarter = modes // 2
+    kept = tab.shape[0] // 2
+    split = kept // 32 * 16
+    pieces = [(0, 0, split), (0, split, kept), (1, 0, split), (1, split, kept)]
     tab_copies = []
-    for i in range(4):
-        rows = pl.ds(i * quarter, quarter)
+    for i, (c, begin, end) in enumerate(pieces):
+        rows = pl.ds(c * kept + begin, end - begin)
         copy = pltpu.make_async_copy(tab_hbm.at[rows], tab.at[rows], tab_sem.at[i])
         copy.start()
         tab_copies.append(copy)
 
     for f in range(2):
-        value = g_ref[f]
+        value = g_ref[:, f, :]
         high = value.astype(jnp.bfloat16).astype(jnp.float32)
         grid[f * DEG : f * DEG + ROWS, :] = high
         grid[64 + f * DEG : 64 + f * DEG + ROWS, :] = value - high
-    both = grid[...].astype(jnp.bfloat16)
+    down = jnp.transpose(grid[...])
+    turn = jnp.where(iota(down.shape, 0) % 2 == 1, -1.0, 1.0)
+    both[...] = jnp.concatenate([down, down * turn], axis=1).astype(jnp.bfloat16)
 
     for t in range(asg_ref.shape[0]):
         row = jnp.broadcast_to(asg_ref[t : t + 1, :].astype(jnp.float32), (LANES, LANES))
         asg_col[t * LANES : (t + 1) * LANES, :] = jnp.transpose(row)
 
-    for i in range(4):
+    for i, (c, begin, end) in enumerate(pieces):
         tab_copies[i].wait()
-        part = dot_nt(tab[i * quarter : (i + 1) * quarter, :], both)
-        total = part + pltpu.roll(part, 64, 1)
-        c, r = i // 2, (i % 2) * quarter
-        spec[r : r + quarter, c * LANES : (c + 1) * LANES] = total.astype(jnp.bfloat16)
+        part = dot(tab[c * kept + begin : c * kept + end, :], both[...])
+        for turned in range(2):
+            half_part = part[:, turned * LANES : (turned + 1) * LANES]
+            total = half_part + pltpu.roll(half_part, 64, 1)
+            if turned and c:
+                total = -total
+            begins = turned * kept + begin
+            spec[begins : begins + end - begin, c * LANES : (c + 1) * LANES] = total.astype(jnp.bfloat16)
 
     picked = 2 * dests
     lane = iota((picked, LANES), 1)
     tiles = -(-modes // LANES)
-    mode_of = iota((picked, modes), 1).astype(jnp.float32)
+    entry = iota((picked, 2 * kept), 1)
+    mirrored = nlon // 2 - (entry - kept)
+    mode_of = jnp.where(entry < kept, entry, jnp.where(mirrored >= kept, mirrored, -1)).astype(jnp.float32)
+    entry_tiles = -(-2 * kept // LANES)
     packed = [[jnp.zeros((picked, LANES), jnp.float32) for _ in range(2)] for _ in range(2)]
     for kappa in range(KAPPA):
         wave = asg_col[pl.ds(kappa, picked, stride=KAPPA), :]
-        wave = jnp.concatenate([wave] * tiles, axis=1)[:, :modes]
+        wave = jnp.concatenate([wave] * entry_tiles, axis=1)[:, : 2 * kept]
         choice = jnp.where(wave == mode_of, 1.0, 0.0).astype(jnp.bfloat16)
         chosen = dot(choice, spec[...])
         here = (lane >= kappa * ROWS) & (lane < (kappa + 1) * ROWS)
@@ -242,21 +254,25 @@
     def contract(p, begin, end):
         arrived = units[begin:end, p * 16 : (p + 1) * 16, :].reshape((end - begin) * 16, wide)
         factor = jnp.concatenate([w_own[p], w_part[p]], axis=0)
-        return dot_nt(factor, arrived).astype(jnp.bfloat16)
-
-    middle = n_z // 2
+        columns = dot_nt(factor, arrived).astype(jnp.bfloat16)
+        return dot(columns, place[begin * 16 : end * 16])
+
+    ends = {n_z // 4: n_z // 2, n_z * 3 // 8: n_z * 3 // 4 + 1, n_z // 2 - 1: last}
+    done = 0
     for step in range(1, n_z // 2):
         for p in range(PAIRS):
             unit_copy(0, 2 * step - 1, p, right).wait_recv()
             pass_right(step, p)
             unit_copy(0, 2 * step, p, left).wait_recv()
             pass_left(step, p)
-            if step == n_z // 4:
-                first[p] = contract(p, 0, middle)
+        if step in ends:
+            for p in range(PAIRS):
+                value = contract(p, done, ends[step])
+                first[p] = value if done == 0 else first[p] + value
+            done = ends[step]
     for p in range(PAIRS):
         unit_copy(0, last, p, right).wait_recv()
-        second = contract(p, middle, n_z)
-        product = dot(jnp.concatenate([first[p], second], axis=1), place)
+        product = first[p] + contract(p, done, n_z)
         width = n_z * 8
         for s in range(2):
             lanes = slice(s * width, (s + 1) * width)
@@ -277,10 +293,10 @@
         out_ref[other * HALF + s] = p_recv[s][:ROWS, :]
 
 
-def table_of(modes, nlon):
-    phase = np.arange(modes, dtype=np.int64)[:, None] * np.arange(nlon, dtype=np.int64)[None, :] % nlon
+def table_of(kept, nlon):
+    phase = np.arange(kept, dtype=np.int64)[:, None] * np.arange(nlon, dtype=np.int64)[None, :] % nlon
     angle = phase * (2.0 * np.pi / nlon)
-    weight = np.where(np.arange(modes) == 0, 1.0, 2.0)[:, None]
+    weight = np.where(np.arange(kept) == 0, 1.0, 2.0)[:, None]
     return np.concatenate([np.cos(angle) * weight, -np.sin(angle) * weight], axis=0)
 
 
@@ -289,20 +305,22 @@
     nlon = grid_gradient.shape[2]
     wide, half, dests = modes, modes // 2, 2 * n_lat
     tiles = -(-modes // LANES)
-    table = jnp.asarray(table_of(modes, nlon).astype(jnp.bfloat16))
+    kept = (nlon // 4 + 16) // 16 * 16
+    table = jnp.asarray(table_of(kept, nlon).astype(jnp.bfloat16))
     rows = jnp.pad(assign, (0, tiles * LANES - modes)).reshape(tiles, LANES)
     vmem = pl.BlockSpec(memory_space=pltpu.VMEM)
     bf16, f32 = jnp.bfloat16, jnp.float32
     dma = pltpu.SemaphoreType.DMA
-    return pl.pallas_call(
+    result = pl.pallas_call(
         functools.partial(kernel, n_lat, n_z),
-        out_shape=jax.ShapeDtypeStruct((ROWS, ROWS, n_z * 8), bf16),
+        out_shape=pltpu.VMEM((ROWS, ROWS, n_z * 8), bf16),
         in_specs=[vmem, vmem, vmem, pl.BlockSpec(memory_space=pltpu.MemorySpace.HBM)],
         out_specs=vmem,
         scratch_shapes=[
-            pltpu.VMEM((2 * modes, nlon), bf16),
+            pltpu.VMEM((2 * kept, nlon), bf16),
             pltpu.VMEM((LANES, nlon), f32),
-            pltpu.VMEM((modes, 2 * LANES), bf16),
+            pltpu.VMEM((nlon, 2 * LANES), bf16),
+            pltpu.VMEM((2 * kept, 2 * LANES), bf16),
             pltpu.VMEM((tiles * LANES, LANES), f32),
             pltpu.VMEM((dests * 8, LANES), f32),
             pltpu.VMEM((dests, 8, LANES), bf16),
@@ -313,7 +331,7 @@
             pltpu.VMEM((PAIRS, 2 * DEG, wide), bf16),
             pltpu.VMEM((PAIRS, 2 * DEG, wide), bf16),
             pltpu.VMEM((n_z, HALF * 8, wide), bf16),
-            pltpu.VMEM((PAIRS, 4 * DEG, n_z * 8), bf16),
+            pltpu.VMEM((PAIRS, 4 * DEG, 2 * n_z * 8), f32),
             pltpu.VMEM((HALF, DEG, n_z * 8), bf16),
             pltpu.VMEM((HALF, DEG, n_z * 8), bf16),
             dma((4,)),
@@ -327,7 +345,18 @@
         ],
         compiler_params=pltpu.CompilerParams(collective_id=0, has_side_effects=True),
         name="spectral_adjoint",
-    )(grid_gradient, legendre, rows, table)
+    )(jnp.transpose(grid_gradient, (1, 0, 2)), legendre, rows, table)
+
+    def hand_on(result_ref, out_ref):
+        out_ref[...] = result_ref[...]
+
+    return pl.pallas_call(
+        hand_on,
+        out_shape=jax.ShapeDtypeStruct(result.shape, result.dtype),
+        in_specs=[vmem],
+        out_specs=vmem,
+        name="hand_on",
+    )(pltpu.with_memory_space_constraint(result, pltpu.VMEM))
 
 
 def solution(mesh):

time: 67.2 us -> 63.6 us (0.946)
  local copies, waits for them, and re-layouts: 3.19 us -> 0 us
    unnamed x2 -> x0, local copies, waits for them, and re-layouts: 3.19 us -> none
    pallas_call x1 -> x2, Pallas kernels: 63.8 us -> 63.4 us  [the longest x1 62.8 us: per_device(): pl.pallas_call(functools.partial(kernel, n_lat, n_z), out_shape=pltpu.VME...]
where the time goes in v2:
time: 63.6 us; the launch traced here: 63.4 us
  Pallas kernels  63.4 us (100%)
    pallas_call x1, Pallas kernels, per_device(): pl.pallas_call(functools.partial(kernel, n_lat, n_z), out_shape=pltpu.VME...  62.8 us

profile of v2, /device:TPU:1, one launch (start us, length us, event | category | flops | bytes accessed | tf_op | source)
XLA Modules:
  0.0 63.4 jit_solution(11135970252989403306)
XLA Ops:
  0.0 62.8 %spectral_adjoint.1.result_ref = bf16[20,20,128]{2,1,0:T(8,128)(2,1)S(1)} custom-call(f32[20,2,1280]{2,1,0:T(2,128)} %bitcast.2, bf16[20,20,320]{2,1,0:T(8,128)(2,1)} %leg_ref.1, s32[5,128]{1,0:T(8,128)} %bitcast.3, bf16[672,1280]{1,0:T(8,128)(2,1)} %constant.1.clone.tab_hbm), custom_call_target="tpu_custom_call" | custom-call | tf_op jit(solution)/shard_map/spectral_adjoint/pallas_call | solution.py:314
  62.8 0.7 %hand_on.1 = bf16[20,20,128]{2,1,0:T(8,128)(2,1)} custom-call(bf16[20,20,128]{2,1,0:T(8,128)(2,1)S(1)} %spectral_adjoint.1.result_ref), custom_call_target="tpu_custom_call" | custom-call | tf_op jit(solution)/shard_map/hand_on/pallas_call | solution.py:353

commit v3 on v2

--- a/solution.py
+++ b/solution.py
@@ -11,9 +11,9 @@
 MESH = pl.DeviceIdType.MESH
 LANES = 128
 ROWS = 20
-HALF = 10
 KAPPA = 5
-PAIRS = HALF // 2
+OWN = 5
+CHUNKS = (pl.ds(0, 3), pl.ds(3, 2))
 DEG = 24
 NT = (((1,), (1,)), ((), ()))
 
@@ -32,8 +32,8 @@
 
 def kernel(
     n_lat, n_z, g_ref, leg_ref, asg_ref, tab_hbm, out_ref,
-    tab, grid, both, spec, asg_col, send32, send, recv, mixed, leg32, w_own, w_send, w_part, units, first, p_send, p_recv,
-    tab_sem, a_send_sem, a_recv_sem, local_sem, w_sems, p_sems, u_send_sem, u_recv_sem,
+    tab, grid, both, spec, asg_col, send32, send, recv, mixed, leg32, l_send, l_recv, spread, factor, units, away, first,
+    p_send, p_recv, tab_sem, a_send_sem, a_recv_sem, local_sem, l_sems, p_sems, u_send_sem, u_recv_sem,
 ):
     modes = n_lat * ROWS
     wide = modes
@@ -44,9 +44,15 @@
     lev = lax.axis_index("lev")
     z, core = lev // 2, lev % 2
     other = 1 - core
-    right = ((z + 1) % n_z) * 2 + core
-    left = ((z + n_z - 1) % n_z) * 2 + core
+    odd = z % 2
+
+    def along(distance):
+        return ((z + distance + n_z) % n_z) * 2 + core
+
+    twin = z + 1 - 2 * odd
     partner = z * 2 + other
+    team = [(partner, other * 2 + odd), (twin * 2 + core, core * 2 + 1 - odd), (twin * 2 + other, other * 2 + 1 - odd)]
+    home = core * 2 + odd
     me = lat * 2 + core
 
     barrier = pltpu.get_barrier_semaphore()
@@ -54,9 +60,10 @@
     def greet(target_lat, target_lev):
         pl.semaphore_signal(barrier, inc=1, device_id={"lat": target_lat, "lev": target_lev}, device_id_type=MESH)
 
-    greet(lat, right)
-    greet(lat, left)
+    for distance in (1, -1, 2, -2):
+        greet(lat, along(distance))
     greet(lat, partner)
+    greet(lat, team[2][0])
 
     def greet_all(step, carry):
         target = (lat + step) % n_lat
@@ -126,7 +133,7 @@
             send32[pl.ds(f * 2 + c, picked, stride=4), :] = packed[f][c]
     send[...] = send32[...].reshape(dests, 8, LANES).astype(jnp.bfloat16)
 
-    pl.semaphore_wait(barrier, 2 * n_lat - 1 + 2)
+    pl.semaphore_wait(barrier, 2 * n_lat - 1 + 5)
 
     def block_to(target_lat, h):
         pltpu.make_async_remote_copy(
@@ -151,44 +158,29 @@
 
     for s in range(ROWS):
         leg32[s * DEG : s * DEG + ROWS, :] = leg_ref[s].astype(jnp.float32)
+    for group in range(4):
+        l_send[group] = leg32[group * OWN * DEG : (group + 1) * OWN * DEG, :].astype(jnp.bfloat16)
+    l_copies = []
+    for i, (device, group) in enumerate(team):
+        copy = pltpu.make_async_remote_copy(
+            src_ref=l_send.at[group], dst_ref=l_recv.at[i], send_sem=l_sems.at[i], recv_sem=l_sems.at[3 + i],
+            device_id={"lat": lat, "lev": device}, device_id_type=MESH,
+        )
+        copy.start()
+        l_copies.append(copy)
+
     row_of = iota((half, wide), 0)
     col_of = iota((half, wide), 1)
     mirror = jnp.where((row_of == col_of) | (row_of + col_of == wide - 1), 1.0, 0.0).astype(jnp.bfloat16)
-    degree = iota((DEG, wide), 0)
-    sign = jnp.where((degree % 2 == 1) & (iota((DEG, wide), 1) >= half), -1.0, 1.0)
-    degree = degree.astype(jnp.float32)
-
-    def factors(h, p, ref):
-        pair = []
-        first_slot = h * HALF + 2 * p
-        source = leg32[pl.ds(pl.multiple_of(first_slot * DEG, 8), 2 * DEG), :].astype(jnp.bfloat16)
-        spread = dot(source, mirror)
-        for s in range(2):
-            wave = asg_col[pl.ds(lat * ROWS + first_slot + s, 1), :]
-            wave = jnp.concatenate([wave] * tiles, axis=1)[:, :modes]
-            limit = jnp.minimum(modes - wave - (lev * ROWS).astype(jnp.float32), float(ROWS))
-            keep = degree < jnp.broadcast_to(limit, (DEG, wide))
-            pair.append(jnp.where(keep, spread[s * DEG : (s + 1) * DEG] * sign, 0.0))
-        ref[p] = jnp.concatenate(pair, axis=0).astype(jnp.bfloat16)
-
-    for p in range(PAIRS):
-        factors(other, p, w_send)
-    w_copy = pltpu.make_async_remote_copy(
-        src_ref=w_send, dst_ref=w_part, send_sem=w_sems.at[0], recv_sem=w_sems.at[1],
-        device_id={"lat": lat, "lev": partner}, device_id_type=MESH,
-    )
-    w_copy.start()
-    for p in range(PAIRS):
-        factors(core, p, w_own)
-
-    src = iota((n_z * 16, 2 * n_z * 8), 0)
-    dst = iota((n_z * 16, 2 * n_z * 8), 1)
-    position, inner = src // 16, src % 16
-    away = (position + 1) // 2
-    from_z = jnp.where(position % 2 == 1, z - away + n_z, z + away) % n_z
-    field = from_z * 4 + (inner % 8) // 2
-    column = (inner // 8) * (n_z * 8) + (inner % 2) * (n_z * 4) + field
+
+    src = iota((n_z * 8, n_z * 8), 0)
+    dst = iota((n_z * 8, n_z * 8), 1)
+    position, inner = src // 8, src % 8
+    distance = (position + 1) // 2
+    from_z = jnp.where(position % 2 == 1, z - distance + n_z, z + distance) % n_z
+    column = (inner % 2) * (n_z * 4) + from_z * 4 + inner // 2
     place = jnp.where(column == dst, 1.0, 0.0).astype(jnp.bfloat16)
+    spread[0] = dot(l_send[home], mirror)
 
     pltpu.make_async_copy(recv.at[pl.ds(0, dests - 1)], recv.at[pl.ds(0, dests - 1)], a_recv_sem).wait()
     own_block.wait()
@@ -201,8 +193,7 @@
 
     lane = iota((8, LANES), 1)
 
-    def side_by_side(slot):
-        u, kappa = slot // KAPPA, slot % KAPPA
+    def side_by_side(u, kappa):
         parts = [jnp.zeros((8, LANES), jnp.float32) for _ in range(tiles)]
         for i in range(n_lat):
             start = i * ROWS
@@ -214,13 +205,12 @@
             parts[t] = jnp.where((lane >= offset) & (lane < offset + ROWS), value, parts[t])
             if offset + ROWS > LANES:
                 parts[t + 1] = jnp.where(lane < offset + ROWS - LANES, value, parts[t + 1])
-        return jnp.concatenate(parts, axis=1)[:, :wide]
+        return jnp.concatenate(parts, axis=1)[:, :wide].astype(jnp.bfloat16)
 
     def unit_copy(source, target, p, device):
-        rows = pl.ds(p * 16, 16)
         return pltpu.make_async_remote_copy(
-            src_ref=units.at[source, rows],
-            dst_ref=units.at[target, rows],
+            src_ref=source.at[CHUNKS[p]],
+            dst_ref=units.at[target, CHUNKS[p]],
             send_sem=u_send_sem,
             recv_sem=u_recv_sem.at[target, p],
             device_id={"lat": lat, "lev": device},
@@ -228,69 +218,89 @@
         )
 
     last = n_z - 1
-
-    def pass_right(step, p):
-        source = 0 if step == 0 else 2 * step - 1
-        if step + 1 < n_z // 2:
-            unit_copy(source, 2 * step + 1, p, right).start()
-        elif step + 1 == n_z // 2 and p < 3:
-            unit_copy(source, last, p, right).start()
-
-    def pass_left(step, p):
-        source = 2 * step
-        if step + 1 < n_z // 2:
-            unit_copy(source, 2 * step + 2, p, left).start()
-        elif step + 1 == n_z // 2 and p >= 3:
-            unit_copy(source, last, p, left).start()
-
-    for p in range(PAIRS):
-        rows = jnp.concatenate([side_by_side(2 * p), side_by_side(2 * p + 1)], axis=0)
-        units[0, p * 16 : (p + 1) * 16, :] = rows.astype(jnp.bfloat16)
-        pass_right(0, p)
-        pass_left(0, p)
-
-    w_copy.wait()
-
-    def contract(p, begin, end):
-        arrived = units[begin:end, p * 16 : (p + 1) * 16, :].reshape((end - begin) * 16, wide)
-        factor = jnp.concatenate([w_own[p], w_part[p]], axis=0)
-        columns = dot_nt(factor, arrived).astype(jnp.bfloat16)
-        return dot(columns, place[begin * 16 : end * 16])
-
-    ends = {n_z // 4: n_z // 2, n_z * 3 // 8: n_z * 3 // 4 + 1, n_z // 2 - 1: last}
+    turns = n_z // 2
+    right, left = along(2), along(-2)
+
+    def arrive_right(t, p):
+        source = 2 * t - 1
+        unit_copy(away, source, p, right).wait_recv()
+        if t + 2 < turns:
+            unit_copy(units.at[source], source + 4, p, right).start()
+        elif t + 2 == turns and p == 0:
+            unit_copy(units.at[source], last, p, right).start()
+
+    def arrive_left(t, p):
+        source = 2 * t
+        unit_copy(away, source, p, left).wait_recv()
+        if t + 2 < turns:
+            unit_copy(units.at[source], source + 4, p, left).start()
+        elif t + 2 == turns and p == 1:
+            unit_copy(units.at[source], last, p, left).start()
+
+    for p, chunk in enumerate(CHUNKS):
+        for kappa in range(chunk.start, chunk.start + chunk.size):
+            units[0, kappa] = side_by_side(odd, kappa)
+        unit_copy(units.at[0], 3, p, right).start()
+        unit_copy(units.at[0], 4, p, left).start()
+        for kappa in range(chunk.start, chunk.start + chunk.size):
+            away[kappa] = side_by_side(1 - odd, kappa)
+        unit_copy(away, 1, p, along(1)).start()
+        unit_copy(away, 2, p, along(-1)).start()
+
+    for i in range(3):
+        l_copies[i].wait()
+        spread[1 + i] = dot(l_recv[i], mirror)
+    degree = iota((DEG, wide), 0)
+    sign = jnp.where((degree % 2 == 1) & (iota((DEG, wide), 1) >= half), -1.0, 1.0)
+    degree = degree.astype(jnp.float32)
+    for s in range(OWN):
+        wave = asg_col[pl.ds(lat * ROWS + home * OWN + s, 1), :]
+        wave = jnp.concatenate([wave] * tiles, axis=1)[:, :modes]
+        rows = []
+        for i, device in enumerate([lev] + [device for device, _ in team]):
+            limit = jnp.minimum(modes - wave - (device * ROWS).astype(jnp.float32), float(ROWS))
+            keep = degree < jnp.broadcast_to(limit, (DEG, wide))
+            rows.append(jnp.where(keep, spread[i, s * DEG : (s + 1) * DEG, :] * sign, 0.0))
+        factor[s] = jnp.concatenate(rows, axis=0).astype(jnp.bfloat16)
+
+    def contract(s, begin, end):
+        arrived = units[begin:end, s].astype(jnp.float32).reshape((end - begin) * 8, wide).astype(jnp.bfloat16)
+        columns = dot_nt(factor[s], arrived).astype(jnp.bfloat16)
+        return dot(columns, place[begin * 8 : end * 8])
+
     done = 0
-    for step in range(1, n_z // 2):
-        for p in range(PAIRS):
-            unit_copy(0, 2 * step - 1, p, right).wait_recv()
-            pass_right(step, p)
-            unit_copy(0, 2 * step, p, left).wait_recv()
-            pass_left(step, p)
-        if step in ends:
-            for p in range(PAIRS):
-                value = contract(p, done, ends[step])
-                first[p] = value if done == 0 else first[p] + value
-            done = ends[step]
-    for p in range(PAIRS):
-        unit_copy(0, last, p, right).wait_recv()
-        product = first[p] + contract(p, done, n_z)
-        width = n_z * 8
-        for s in range(2):
-            lanes = slice(s * width, (s + 1) * width)
-            mine = product[s * DEG : s * DEG + ROWS, lanes].astype(jnp.bfloat16)
-            out_ref[core * HALF + 2 * p + s] = mine
-            theirs = product[(2 + s) * DEG : (3 + s) * DEG, lanes].astype(jnp.bfloat16)
-            p_send[2 * p + s] = theirs
-
-    p_copy = pltpu.make_async_remote_copy(
-        src_ref=p_send, dst_ref=p_recv, send_sem=p_sems.at[0], recv_sem=p_sems.at[1],
-        device_id={"lat": lat, "lev": partner}, device_id_type=MESH,
-    )
-    p_copy.start()
+    for t in range(1, turns):
+        for p in range(2):
+            arrive_right(t, p)
+            arrive_left(t, p)
+        if t in (n_z // 4, n_z * 3 // 8, turns - 1):
+            end = (2 * t + 1) // 2 * 2
+            for s in range(OWN):
+                value = contract(s, done, end)
+                first[s] = value if done == 0 else first[s] + value
+            done = end
+    for p, chunk in enumerate(CHUNKS):
+        unit_copy(away, last, p, right).wait_recv()
+        for s in range(chunk.start, chunk.start + chunk.size):
+            product = first[s] + contract(s, done, n_z)
+            out_ref[home * OWN + s] = product[:ROWS].astype(jnp.bfloat16)
+            for i in range(3):
+                p_send[i, s] = product[(1 + i) * DEG : (2 + i) * DEG].astype(jnp.bfloat16)
+
+    p_copies = []
+    for i in (2, 1, 0):
+        copy = pltpu.make_async_remote_copy(
+            src_ref=p_send.at[i], dst_ref=p_recv.at[i], send_sem=p_sems.at[i], recv_sem=p_sems.at[3 + i],
+            device_id={"lat": lat, "lev": team[i][0]}, device_id_type=MESH,
+        )
+        copy.start()
+        p_copies.append((i, copy))
     pltpu.make_async_copy(send.at[pl.ds(0, dests - 1)], send.at[pl.ds(0, dests - 1)], a_send_sem).wait()
     pltpu.make_async_copy(units.at[pl.ds(0, last)], units.at[pl.ds(0, last)], u_send_sem).wait()
-    p_copy.wait()
-    for s in range(HALF):
-        out_ref[other * HALF + s] = p_recv[s][:ROWS, :]
+    for i, copy in reversed(p_copies):
+        copy.wait()
+        for s in range(OWN):
+            out_ref[team[i][1] * OWN + s] = p_recv[i, s][:ROWS, :]
 
 
 def table_of(kept, nlon):
@@ -327,21 +337,23 @@
             pltpu.VMEM((dests, 8, LANES), bf16),
             pltpu.VMEM((2, n_lat, 8, LANES), f32),
             pltpu.VMEM((ROWS * DEG, half), f32),
-            pltpu.VMEM((PAIRS, 2 * DEG, wide), bf16),
-            pltpu.VMEM((PAIRS, 2 * DEG, wide), bf16),
-            pltpu.VMEM((PAIRS, 2 * DEG, wide), bf16),
-            pltpu.VMEM((n_z, HALF * 8, wide), bf16),
-            pltpu.VMEM((PAIRS, 4 * DEG, 2 * n_z * 8), f32),
-            pltpu.VMEM((HALF, DEG, n_z * 8), bf16),
-            pltpu.VMEM((HALF, DEG, n_z * 8), bf16),
+            pltpu.VMEM((4, OWN * DEG, half), bf16),
+            pltpu.VMEM((3, OWN * DEG, half), bf16),
+            pltpu.VMEM((4, OWN * DEG, wide), f32),
+            pltpu.VMEM((OWN, 4 * DEG, wide), bf16),
+            pltpu.VMEM((n_z, OWN, 8, wide), bf16),
+            pltpu.VMEM((OWN, 8, wide), bf16),
+            pltpu.VMEM((OWN, 4 * DEG, n_z * 8), f32),
+            pltpu.VMEM((3, OWN, DEG, n_z * 8), bf16),
+            pltpu.VMEM((3, OWN, DEG, n_z * 8), bf16),
             dma((4,)),
             dma,
             dma,
             dma,
-            dma((2,)),
-            dma((2,)),
+            dma((6,)),
+            dma((6,)),
             dma,
-            dma((n_z, PAIRS)),
+            dma((n_z, 2)),
         ],
         compiler_params=pltpu.CompilerParams(collective_id=0, has_side_effects=True),
         name="spectral_adjoint",

time: 63.6 us -> 58.7 us (0.923)
  Pallas kernels: 63.4 us -> 58.5 us
    pallas_call x1, Pallas kernels: 62.8 us -> 57.9 us  [per_device(): pl.pallas_call(functools.partial(kernel, n_lat, n_z), out_shape=pltpu.VME...]
where the time goes in v3:
time: 58.7 us; the launch traced here: 58.5 us
  Pallas kernels  58.5 us (100%)
    pallas_call x1, Pallas kernels, per_device(): pl.pallas_call(functools.partial(kernel, n_lat, n_z), out_shape=pltpu.VME...  57.9 us

profile of v3, /device:TPU:1, one launch (start us, length us, event | category | flops | bytes accessed | tf_op | source)
XLA Modules:
  0.0 58.5 jit_solution(6510975418080281477)
XLA Ops:
  0.0 57.9 %spectral_adjoint.1.result_ref = bf16[20,20,128]{2,1,0:T(8,128)(2,1)S(1)} custom-call(f32[20,2,1280]{2,1,0:T(2,128)} %bitcast.2, bf16[20,20,320]{2,1,0:T(8,128)(2,1)} %leg_ref.1, s32[5,128]{1,0:T(8,128)} %bitcast.3, bf16[672,1280]{1,0:T(8,128)(2,1)} %constant.1.clone.tab_hbm), custom_call_target="tpu_custom_call" | custom-call | tf_op jit(solution)/shard_map/spectral_adjoint/pallas_call | solution.py:324
  57.9 0.7 %hand_on.1 = bf16[20,20,128]{2,1,0:T(8,128)(2,1)} custom-call(bf16[20,20,128]{2,1,0:T(8,128)(2,1)S(1)} %spectral_adjoint.1.result_ref), custom_call_target="tpu_custom_call" | custom-call | tf_op jit(solution)/shard_map/hand_on/pallas_call | solution.py:365

commit v4 on v3

--- a/solution.py
+++ b/solution.py
@@ -32,7 +32,7 @@
 
 def kernel(
     n_lat, n_z, g_ref, leg_ref, asg_ref, tab_hbm, out_ref,
-    tab, grid, both, spec, asg_col, send32, send, recv, mixed, leg32, l_send, l_recv, spread, factor, units, away, first,
+    tab, grid, both, spec, choice, asg_col, send32, send, recv, mixed, leg32, l_send, l_recv, spread, factor, units, away, first,
     p_send, p_recv, tab_sem, a_send_sem, a_recv_sem, local_sem, l_sems, p_sems, u_send_sem, u_recv_sem,
 ):
     modes = n_lat * ROWS
@@ -55,24 +55,6 @@
     home = core * 2 + odd
     me = lat * 2 + core
 
-    barrier = pltpu.get_barrier_semaphore()
-
-    def greet(target_lat, target_lev):
-        pl.semaphore_signal(barrier, inc=1, device_id={"lat": target_lat, "lev": target_lev}, device_id_type=MESH)
-
-    for distance in (1, -1, 2, -2):
-        greet(lat, along(distance))
-    greet(lat, partner)
-    greet(lat, team[2][0])
-
-    def greet_all(step, carry):
-        target = (lat + step) % n_lat
-        greet(target, z * 2)
-        greet(target, z * 2 + 1)
-        return carry
-
-    lax.fori_loop(1, n_lat, greet_all, 0)
-
     kept = tab.shape[0] // 2
     split = kept // 32 * 16
     pieces = [(0, 0, split), (0, split, kept), (1, 0, split), (1, split, kept)]
@@ -83,6 +65,20 @@
         copy.start()
         tab_copies.append(copy)
 
+    barrier = pltpu.get_barrier_semaphore()
+
+    def greet(target_lat, target_lev):
+        pl.semaphore_signal(barrier, inc=1, device_id={"lat": target_lat, "lev": target_lev}, device_id_type=MESH)
+
+    for distance in (1, -1, 2, -2):
+        greet(lat, along(distance))
+    greet(lat, partner)
+    greet(lat, team[2][0])
+
+    for step in range(1, n_lat):
+        greet((lat + step) % n_lat, z * 2)
+        greet((lat + step) % n_lat, z * 2 + 1)
+
     for f in range(2):
         value = g_ref[:, f, :]
         high = value.astype(jnp.bfloat16).astype(jnp.float32)
@@ -95,6 +91,18 @@
     for t in range(asg_ref.shape[0]):
         row = jnp.broadcast_to(asg_ref[t : t + 1, :].astype(jnp.float32), (LANES, LANES))
         asg_col[t * LANES : (t + 1) * LANES, :] = jnp.transpose(row)
+
+    picked = 2 * dests
+    lane = iota((picked, LANES), 1)
+    tiles = -(-modes // LANES)
+    entry = iota((picked, 2 * kept), 1)
+    mirrored = nlon // 2 - (entry - kept)
+    mode_of = jnp.where(entry < kept, entry, jnp.where(mirrored >= kept, mirrored, -1)).astype(jnp.float32)
+    entry_tiles = -(-2 * kept // LANES)
+    for kappa in range(KAPPA):
+        wave = asg_col[pl.ds(kappa, picked, stride=KAPPA), :]
+        wave = jnp.concatenate([wave] * entry_tiles, axis=1)[:, : 2 * kept]
+        choice[kappa] = jnp.where(wave == mode_of, 1.0, 0.0).astype(jnp.bfloat16)
 
     for i, (c, begin, end) in enumerate(pieces):
         tab_copies[i].wait()
@@ -107,19 +115,9 @@
             begins = turned * kept + begin
             spec[begins : begins + end - begin, c * LANES : (c + 1) * LANES] = total.astype(jnp.bfloat16)
 
-    picked = 2 * dests
-    lane = iota((picked, LANES), 1)
-    tiles = -(-modes // LANES)
-    entry = iota((picked, 2 * kept), 1)
-    mirrored = nlon // 2 - (entry - kept)
-    mode_of = jnp.where(entry < kept, entry, jnp.where(mirrored >= kept, mirrored, -1)).astype(jnp.float32)
-    entry_tiles = -(-2 * kept // LANES)
     packed = [[jnp.zeros((picked, LANES), jnp.float32) for _ in range(2)] for _ in range(2)]
     for kappa in range(KAPPA):
-        wave = asg_col[pl.ds(kappa, picked, stride=KAPPA), :]
-        wave = jnp.concatenate([wave] * entry_tiles, axis=1)[:, : 2 * kept]
-        choice = jnp.where(wave == mode_of, 1.0, 0.0).astype(jnp.bfloat16)
-        chosen = dot(choice, spec[...])
+        chosen = dot(choice[kappa], spec[...])
         here = (lane >= kappa * ROWS) & (lane < (kappa + 1) * ROWS)
         for f in range(2):
             for c in range(2):
@@ -273,7 +271,7 @@
         for p in range(2):
             arrive_right(t, p)
             arrive_left(t, p)
-        if t in (n_z // 4, n_z * 3 // 8, turns - 1):
+        if t in (turns - 2, turns - 1):
             end = (2 * t + 1) // 2 * 2
             for s in range(OWN):
                 value = contract(s, done, end)
@@ -331,6 +329,7 @@
             pltpu.VMEM((LANES, nlon), f32),
             pltpu.VMEM((nlon, 2 * LANES), bf16),
             pltpu.VMEM((2 * kept, 2 * LANES), bf16),
+            pltpu.VMEM((KAPPA, 2 * dests, 2 * kept), bf16),
             pltpu.VMEM((tiles * LANES, LANES), f32),
             pltpu.VMEM((dests * 8, LANES), f32),
             pltpu.VMEM((dests, 8, LANES), bf16),

time: 58.7 us -> 56.6 us (0.964)
  Pallas kernels: 58.5 us -> 56 us
    pallas_call x1, Pallas kernels: 57.9 us -> 55.3 us  [per_device(): pl.pallas_call(functools.partial(kernel, n_lat, n_z), out_shape=pltpu.VME...]
where the time goes in v4:
time: 56.6 us; the launch traced here: 56 us
  Pallas kernels  56 us (99%)
    pallas_call x1, Pallas kernels, per_device(): pl.pallas_call(functools.partial(kernel, n_lat, n_z), out_shape=pltpu.VME...  55.3 us

profile of v4, /device:TPU:1, one launch (start us, length us, event | category | flops | bytes accessed | tf_op | source)
XLA Modules:
  0.0 56.0 jit_solution(673651189602902796)
XLA Ops:
  0.0 55.3 %spectral_adjoint.1.result_ref = bf16[20,20,128]{2,1,0:T(8,128)(2,1)S(1)} custom-call(f32[20,2,1280]{2,1,0:T(2,128)} %bitcast.2, bf16[20,20,320]{2,1,0:T(8,128)(2,1)} %leg_ref.1, s32[5,128]{1,0:T(8,128)} %bitcast.3, bf16[672,1280]{1,0:T(8,128)(2,1)} %constant.1.clone.tab_hbm), custom_call_target="tpu_custom_call" | custom-call | tf_op jit(solution)/shard_map/spectral_adjoint/pallas_call | solution.py:322
  55.3 0.7 %hand_on.1 = bf16[20,20,128]{2,1,0:T(8,128)(2,1)} custom-call(bf16[20,20,128]{2,1,0:T(8,128)(2,1)S(1)} %spectral_adjoint.1.result_ref), custom_call_target="tpu_custom_call" | custom-call | tf_op jit(solution)/shard_map/hand_on/pallas_call | solution.py:364

commit v5 on v4

--- a/solution.py
+++ b/solution.py
@@ -31,9 +31,9 @@
 
 
 def kernel(
-    n_lat, n_z, g_ref, leg_ref, asg_ref, tab_hbm, out_ref,
-    tab, grid, both, spec, choice, asg_col, send32, send, recv, mixed, leg32, l_send, l_recv, spread, factor, units, away, first,
-    p_send, p_recv, tab_sem, a_send_sem, a_recv_sem, local_sem, l_sems, p_sems, u_send_sem, u_recv_sem,
+    n_lat, n_z, g_ref, leg_hbm, asg_ref, tab_hbm, out_ref,
+    tab, leg, grid, both, spec, choice, asg_col, send32, send, recv, mixed, leg32, l_send, l_recv, spread, factor, units, away, first,
+    p_send, p_recv, tab_sem, a_send_sem, a_recv_sem, local_sem, l_sems, p_sems, u_send_sem, u_recv_sem, leg_sem,
 ):
     modes = n_lat * ROWS
     wide = modes
@@ -64,6 +64,8 @@
         copy = pltpu.make_async_copy(tab_hbm.at[rows], tab.at[rows], tab_sem.at[i])
         copy.start()
         tab_copies.append(copy)
+    leg_copy = pltpu.make_async_copy(leg_hbm, leg, leg_sem)
+    leg_copy.start()
 
     barrier = pltpu.get_barrier_semaphore()
 
@@ -154,8 +156,9 @@
     own_block = pltpu.make_async_copy(send.at[me], recv.at[me], local_sem)
     own_block.start()
 
+    leg_copy.wait()
     for s in range(ROWS):
-        leg32[s * DEG : s * DEG + ROWS, :] = leg_ref[s].astype(jnp.float32)
+        leg32[s * DEG : s * DEG + ROWS, :] = leg[s].astype(jnp.float32)
     for group in range(4):
         l_send[group] = leg32[group * OWN * DEG : (group + 1) * OWN * DEG, :].astype(jnp.bfloat16)
     l_copies = []
@@ -245,21 +248,22 @@
         unit_copy(away, 1, p, along(1)).start()
         unit_copy(away, 2, p, along(-1)).start()
 
-    for i in range(3):
-        l_copies[i].wait()
-        spread[1 + i] = dot(l_recv[i], mirror)
-    degree = iota((DEG, wide), 0)
-    sign = jnp.where((degree % 2 == 1) & (iota((DEG, wide), 1) >= half), -1.0, 1.0)
-    degree = degree.astype(jnp.float32)
-    for s in range(OWN):
-        wave = asg_col[pl.ds(lat * ROWS + home * OWN + s, 1), :]
-        wave = jnp.concatenate([wave] * tiles, axis=1)[:, :modes]
-        rows = []
-        for i, device in enumerate([lev] + [device for device, _ in team]):
-            limit = jnp.minimum(modes - wave - (device * ROWS).astype(jnp.float32), float(ROWS))
-            keep = degree < jnp.broadcast_to(limit, (DEG, wide))
-            rows.append(jnp.where(keep, spread[i, s * DEG : (s + 1) * DEG, :] * sign, 0.0))
-        factor[s] = jnp.concatenate(rows, axis=0).astype(jnp.bfloat16)
+    def prepare_factors():
+        for i in range(3):
+            l_copies[i].wait()
+            spread[1 + i] = dot(l_recv[i], mirror)
+        degree = iota((DEG, wide), 0)
+        sign = jnp.where((degree % 2 == 1) & (iota((DEG, wide), 1) >= half), -1.0, 1.0)
+        degree = degree.astype(jnp.float32)
+        for s in range(OWN):
+            wave = asg_col[pl.ds(lat * ROWS + home * OWN + s, 1), :]
+            wave = jnp.concatenate([wave] * tiles, axis=1)[:, :modes]
+            rows = []
+            for i, device in enumerate([lev] + [device for device, _ in team]):
+                limit = jnp.minimum(modes - wave - (device * ROWS).astype(jnp.float32), float(ROWS))
+                keep = degree < jnp.broadcast_to(limit, (DEG, wide))
+                rows.append(jnp.where(keep, spread[i, s * DEG : (s + 1) * DEG, :] * sign, 0.0))
+            factor[s] = jnp.concatenate(rows, axis=0).astype(jnp.bfloat16)
 
     def contract(s, begin, end):
         arrived = units[begin:end, s].astype(jnp.float32).reshape((end - begin) * 8, wide).astype(jnp.bfloat16)
@@ -271,6 +275,8 @@
         for p in range(2):
             arrive_right(t, p)
             arrive_left(t, p)
+        if t == 2:
+            prepare_factors()
         if t in (turns - 2, turns - 1):
             end = (2 * t + 1) // 2 * 2
             for s in range(OWN):
@@ -317,15 +323,17 @@
     table = jnp.asarray(table_of(kept, nlon).astype(jnp.bfloat16))
     rows = jnp.pad(assign, (0, tiles * LANES - modes)).reshape(tiles, LANES)
     vmem = pl.BlockSpec(memory_space=pltpu.VMEM)
+    hbm = pl.BlockSpec(memory_space=pltpu.MemorySpace.HBM)
     bf16, f32 = jnp.bfloat16, jnp.float32
     dma = pltpu.SemaphoreType.DMA
     result = pl.pallas_call(
         functools.partial(kernel, n_lat, n_z),
         out_shape=pltpu.VMEM((ROWS, ROWS, n_z * 8), bf16),
-        in_specs=[vmem, vmem, vmem, pl.BlockSpec(memory_space=pltpu.MemorySpace.HBM)],
+        in_specs=[vmem, hbm, vmem, hbm],
         out_specs=vmem,
         scratch_shapes=[
             pltpu.VMEM((2 * kept, nlon), bf16),
+            pltpu.VMEM((ROWS, ROWS, half), bf16),
             pltpu.VMEM((LANES, nlon), f32),
             pltpu.VMEM((nlon, 2 * LANES), bf16),
             pltpu.VMEM((2 * kept, 2 * LANES), bf16),
@@ -353,6 +361,7 @@
             dma((6,)),
             dma,
             dma((n_z, 2)),
+            dma,
         ],
         compiler_params=pltpu.CompilerParams(collective_id=0, has_side_effects=True),
         name="spectral_adjoint",

time: 56.6 us -> 56.5 us (level)
  no operation moved by 1% of the time
where the time goes in v5:
time: 56.5 us; the launch traced here: 55.6 us
  Pallas kernels  55.6 us (98%)
    pallas_call x1, Pallas kernels, per_device(): pl.pallas_call(functools.partial(kernel, n_lat, n_z), out_shape=pltpu.VME...  54.9 us

profile of v5, /device:TPU:1, one launch (start us, length us, event | category | flops | bytes accessed | tf_op | source)
XLA Modules:
  0.0 55.6 jit_solution(5463693493912744451)
XLA Ops:
  0.0 54.9 %spectral_adjoint.1.result_ref = bf16[20,20,128]{2,1,0:T(8,128)(2,1)S(1)} custom-call(f32[20,2,1280]{2,1,0:T(2,128)} %bitcast.2, bf16[20,20,320]{2,1,0:T(8,128)(2,1)} %leg_hbm.1, s32[5,128]{1,0:T(8,128)} %bitcast.3, bf16[672,1280]{1,0:T(8,128)(2,1)} %constant.1.clone.tab_hbm), custom_call_target="tpu_custom_call" | custom-call | tf_op jit(solution)/shard_map/spectral_adjoint/pallas_call | solution.py:329
  54.9 0.7 %hand_on.1 = bf16[20,20,128]{2,1,0:T(8,128)(2,1)} custom-call(bf16[20,20,128]{2,1,0:T(8,128)(2,1)S(1)} %spectral_adjoint.1.result_ref), custom_call_target="tpu_custom_call" | custom-call | tf_op jit(solution)/shard_map/hand_on/pallas_call | solution.py:373

commit v6 on v5

--- a/solution.py
+++ b/solution.py
@@ -283,6 +283,7 @@
                 value = contract(s, done, end)
                 first[s] = value if done == 0 else first[s] + value
             done = end
+    p_copies = []
     for p, chunk in enumerate(CHUNKS):
         unit_copy(away, last, p, right).wait_recv()
         for s in range(chunk.start, chunk.start + chunk.size):
@@ -290,20 +291,21 @@
             out_ref[home * OWN + s] = product[:ROWS].astype(jnp.bfloat16)
             for i in range(3):
                 p_send[i, s] = product[(1 + i) * DEG : (2 + i) * DEG].astype(jnp.bfloat16)
-
-    p_copies = []
-    for i in (2, 1, 0):
-        copy = pltpu.make_async_remote_copy(
-            src_ref=p_send.at[i], dst_ref=p_recv.at[i], send_sem=p_sems.at[i], recv_sem=p_sems.at[3 + i],
-            device_id={"lat": lat, "lev": team[i][0]}, device_id_type=MESH,
-        )
-        copy.start()
-        p_copies.append((i, copy))
+        for i in (2, 1, 0):
+            copy = pltpu.make_async_remote_copy(
+                src_ref=p_send.at[i, chunk], dst_ref=p_recv.at[i, chunk],
+                send_sem=p_sems.at[p, i], recv_sem=p_sems.at[p, 3 + i],
+                device_id={"lat": lat, "lev": team[i][0]}, device_id_type=MESH,
+            )
+            copy.start()
+            p_copies.append((i, chunk, copy))
+
+
     pltpu.make_async_copy(send.at[pl.ds(0, dests - 1)], send.at[pl.ds(0, dests - 1)], a_send_sem).wait()
     pltpu.make_async_copy(units.at[pl.ds(0, last)], units.at[pl.ds(0, last)], u_send_sem).wait()
-    for i, copy in reversed(p_copies):
+    for i, chunk, copy in p_copies:
         copy.wait()
-        for s in range(OWN):
+        for s in range(chunk.start, chunk.start + chunk.size):
             out_ref[team[i][1] * OWN + s] = p_recv[i, s][:ROWS, :]
 
 
@@ -358,7 +360,7 @@
             dma,
             dma,
             dma((6,)),
-            dma((6,)),
+            dma((2, 6)),
             dma,
             dma((n_z, 2)),
             dma,

time: 56.5 us -> 56.2 us (level)
  no operation moved by 1% of the time
where the time goes in v6:
time: 56.2 us; the launch traced here: 55.4 us
  Pallas kernels  55.4 us (99%)
    pallas_call x1, Pallas kernels, per_device(): pl.pallas_call(functools.partial(kernel, n_lat, n_z), out_shape=pltpu.VME...  54.7 us

profile of v6, /device:TPU:1, one launch (start us, length us, event | category | flops | bytes accessed | tf_op | source)
XLA Modules:
  0.0 55.4 jit_solution(8635018741082955777)
XLA Ops:
  0.0 54.7 %spectral_adjoint.1.result_ref = bf16[20,20,128]{2,1,0:T(8,128)(2,1)S(1)} custom-call(f32[20,2,1280]{2,1,0:T(2,128)} %bitcast.2, bf16[20,20,320]{2,1,0:T(8,128)(2,1)} %leg_hbm.1, s32[5,128]{1,0:T(8,128)} %bitcast.3, bf16[672,1280]{1,0:T(8,128)(2,1)} %constant.1.clone.tab_hbm), custom_call_target="tpu_custom_call" | custom-call | tf_op jit(solution)/shard_map/spectral_adjoint/pallas_call | solution.py:331
  54.7 0.7 %hand_on.1 = bf16[20,20,128]{2,1,0:T(8,128)(2,1)} custom-call(bf16[20,20,128]{2,1,0:T(8,128)(2,1)S(1)} %spectral_adjoint.1.result_ref), custom_call_target="tpu_custom_call" | custom-call | tf_op jit(solution)/shard_map/hand_on/pallas_call | solution.py:375
